TPU v7x, 32 devices: a whole 2x2x4 slice. The times are simulated.
32 devices in a mesh: section: 4 (over x, core), sp: 8 (over z, y).
Axes of the slice: x: 2, y: 2, z: 4, core: 2. Of those that a mesh axis runs over, the one named last changes fastest.
Arguments:
- field_in: bfloat16 [4, 384, 192, 768], P('section', 'sp'), may hold values from -6 to 6
- spectral_gain: bfloat16 [4, 192], P('section'), may hold values from 0.5 to 1.5
- spectral_weight: bfloat16 [4, 384, 192, 384], P('section', 'sp'), may hold values from -0.3125 to 0.3125
- mixer_gain: bfloat16 [4, 192], P('section'), may hold values from 0.5 to 1.5
- up_weight: bfloat16 [4, 192, 384], P('section'), may hold values from -0.4375 to 0.4375
- up_bias: bfloat16 [4, 384], P('section'), may hold values from -3 to 3
- down_weight: bfloat16 [4, 192, 384], P('section'), may hold values from -0.3125 to 0.3125
Outputs:
- next_field: bfloat16 [4, 384, 192, 768], P('section', 'sp')
All inputs are finite; a program needn't handle non-finite values.
Results may differ from a plain program's by a relative error of at most 0.012.
Values may be sent and summed in bfloat16 or wider, within the bound.
A program may use at most 192 MiB of HBM per device.

v0:
```python
import math
import jax
import jax.numpy as jnp
from jax import lax
from jax.sharding import PartitionSpec as P

C = 192
NLAT = 384
NLON = 768
LMAX = 384
MMAX = 384
CHUNKS = 4
EPSILON = 1e-05


def passed_along(value, axis, by):
    count = lax.axis_size(axis)
    return lax.ppermute(value, axis, [(i, (i + by) % count) for i in range(count)])


def quad_weights(cycle_index, cycle_count):
    terms_count = cycle_count // 2
    orders = jnp.arange(1, terms_count + 1, dtype=jnp.int32)
    phase_turns = orders[None, :] * (2 * cycle_index[:, None] + 1) % (2 * cycle_count)
    angles = math.pi * phase_turns.astype(jnp.float32) / cycle_count
    orders_real = orders.astype(jnp.float32)
    series = jnp.sum(jnp.cos(angles) / (4.0 * orders_real * orders_real - 1.0)[None, :], axis=1)
    return 2.0 / cycle_count * (1.0 - 2.0 * series)


def fourier_tables(point_count, orders):
    points = jnp.arange(point_count, dtype=jnp.int32)
    phase_turns = points[:, None] * orders[None, :] % point_count
    angles = 2.0 * math.pi / point_count * phase_turns.astype(jnp.float32)
    cosines = jnp.cos(angles)
    sine_values = jnp.sin(angles)
    forward = jnp.stack([cosines, -sine_values], axis=1).astype(jnp.bfloat16)
    doubling = jnp.where(orders == 0, 1.0, 2.0).astype(jnp.float32)[:, None]
    inverse = jnp.stack([cosines.T * doubling, -sine_values.T * doubling], axis=0).astype(
        jnp.bfloat16
    )
    return (forward, inverse)


def step_entries(degree, order_col, cosines):
    active = degree >= order_col + 1.0
    further = degree >= order_col + 2.0
    degree_sq = degree * degree
    order_sq = order_col * order_col
    lead_coeff = jnp.sqrt(
        jnp.where(
            active, (4.0 * degree_sq - 1.0) / jnp.where(active, degree_sq - order_sq, 1.0), 0.0
        )
    )
    before = degree - 1.0
    before_sq = before * before
    trail_coeff = jnp.sqrt(
        jnp.where(
            further, (before_sq - order_sq) / jnp.where(further, 4.0 * before_sq - 1.0, 1.0), 0.0
        )
    )
    diag_top = jnp.where(active, lead_coeff * cosines, 1.0)
    off_top = jnp.where(active, -lead_coeff * trail_coeff, 0.0)
    off_low = jnp.where(active, 1.0, 0.0)
    diag_low = jnp.where(active, 0.0, 1.0)
    return (diag_top, off_top, off_low, diag_low)


def legendre_rows(order_index, cycle_count, degree_count):
    colatitude = math.pi * (jnp.arange(cycle_count, dtype=jnp.float32) + 0.5) / cycle_count
    cosines = jnp.cos(colatitude)[None, None, :]
    sine_values = jnp.sin(colatitude)
    order_real = order_index.astype(jnp.float32)
    steps_all = jnp.arange(1, degree_count + 1, dtype=jnp.float32)
    factors = jnp.log((2.0 * steps_all - 1.0) / (2.0 * steps_all))
    below_mask = (steps_all[None, :] <= order_real[:, None]).astype(jnp.float32)
    partial_log = jnp.sum(below_mask * factors[None, :], axis=1)
    start_log = 0.5 * jnp.log((2.0 * order_real + 1.0) / (4.0 * math.pi)) + 0.5 * partial_log
    start_log = start_log[:, None] + order_real[:, None] * jnp.log(sine_values)[None, :]
    order_col = order_real[None, :, None]
    block_count = degree_count // 16
    block_base = (16 * jnp.arange(block_count, dtype=jnp.int32)).astype(jnp.float32)[:, None, None]
    shape_all = (block_count, order_index.shape[0], cycle_count)
    unit_array = jnp.ones(shape_all, jnp.float32)
    zero_array = jnp.zeros(shape_all, jnp.float32)

    def product_half(half_turn, matrices):
        upper_left, upper_right, lower_left, lower_right, log_scale = matrices
        for inner_step in range(8):
            degree = block_base + (half_turn * 8 + inner_step).astype(jnp.float32)
            diag_top, off_top, off_low, diag_low = step_entries(degree, order_col, cosines)
            next_ul = diag_top * upper_left + off_top * lower_left
            next_ur = diag_top * upper_right + off_top * lower_right
            next_ll = off_low * upper_left + diag_low * lower_left
            next_lr = off_low * upper_right + diag_low * lower_right
            largest = jnp.maximum(
                jnp.maximum(jnp.abs(next_ul), jnp.abs(next_ur)),
                jnp.maximum(jnp.abs(next_ll), jnp.abs(next_lr)),
            )
            upper_left = next_ul / largest
            upper_right = next_ur / largest
            lower_left = next_ll / largest
            lower_right = next_lr / largest
            log_scale = log_scale + jnp.log(largest)
        return (upper_left, upper_right, lower_left, lower_right, log_scale)

    products = lax.fori_loop(
        0, 2, product_half, (unit_array, zero_array, zero_array, unit_array, zero_array)
    )

    def carry_block(vector_state, block_matrix):
        lead_value, lag_value, log_value = vector_state
        upper_left, upper_right, lower_left, lower_right, log_scale = block_matrix
        next_lead = upper_left * lead_value + upper_right * lag_value
        next_lag = lower_left * lead_value + lower_right * lag_value
        largest = jnp.maximum(jnp.abs(next_lead), jnp.abs(next_lag))
        return (
            (next_lead / largest, next_lag / largest, log_value + log_scale + jnp.log(largest)),
            vector_state,
        )

    initial = (unit_array[0], zero_array[0], start_log)
    final_state, starts = lax.scan(carry_block, initial, products)

    def degree_half(vector_state, half_turn):
        lead_value, lag_value, log_value = vector_state
        values = []
        for inner_step in range(8):
            degree = block_base + (half_turn * 8 + inner_step).astype(jnp.float32)
            diag_top, off_top, off_low, diag_low = step_entries(degree, order_col, cosines)
            next_lead = diag_top * lead_value + off_top * lag_value
            next_lag = off_low * lead_value + diag_low * lag_value
            largest = jnp.maximum(jnp.abs(next_lead), jnp.abs(next_lag))
            lead_value = next_lead / largest
            lag_value = next_lag / largest
            log_value = log_value + jnp.log(largest)
            values.append(lead_value * jnp.exp(log_value))
        return ((lead_value, lag_value, log_value), jnp.stack(values))

    last_state, table_rows = lax.scan(degree_half, starts, jnp.arange(2, dtype=jnp.int32))
    legendre = jnp.transpose(table_rows, (3, 2, 0, 1, 4)).reshape(
        order_index.shape[0], degree_count, cycle_count
    )
    degrees = jnp.arange(degree_count, dtype=jnp.int32)
    return jnp.where(degrees[None, :, None] >= order_index[:, None, None], legendre, 0.0)


def layer_norm(values, gain_row):
    values = values.astype(jnp.float32)
    average = jnp.mean(values, axis=-2, keepdims=True)
    centred = values - average
    variance = jnp.mean(centred * centred, axis=-2, keepdims=True)
    return centred * lax.rsqrt(variance + EPSILON) * gain_row.astype(jnp.float32)[:, None]


def mixing_matrix(weight):
    width = weight.shape[1]
    real_weight = weight[:, :, :width]
    imag_weight = weight[:, :, width:]
    top_half = jnp.concatenate([real_weight, imag_weight], axis=2)
    bottom_half = jnp.concatenate([-imag_weight, real_weight], axis=2)
    return jnp.concatenate([top_half, bottom_half], axis=1)


def order_list(sp_count, modes_dev):
    slots = jnp.arange(MMAX, dtype=jnp.int32)
    owner = slots // modes_dev
    within = slots % modes_dev
    mirrored = jnp.where(within % 2 == 0, owner, sp_count - 1 - owner)
    return within * sp_count + mirrored


def triangle_plan(sp_count, half):
    plan = []
    for rank in range(sp_count):
        low_block = min(rank, sp_count - 1 - rank)
        high_block = sp_count - 1 - low_block
        low_half = 0 if rank == low_block else 1
        low_start = (2 * low_block + low_half) * half
        high_start = (2 * high_block + 1 - low_half) * half
        low_count = (low_start + half - 1) // sp_count + 1
        high_count = (high_start + half - 1) // sp_count + 1
        plan.append((low_start, low_count, high_start, high_count))
    slots = max((entry[1] + entry[3] for entry in plan))
    return (plan, slots)


def shards(field_in, spectral_gain, spectral_weight, mixer_gain, up_weight, up_bias, down_weight):
    grid_values = field_in[0]
    cycle_rows = grid_values.shape[0]
    sp_count = lax.axis_size("sp")
    device_rank = lax.axis_index("sp")
    modes_dev = MMAX // sp_count
    all_orders = order_list(sp_count, modes_dev)
    order_index = lax.dynamic_slice_in_dim(all_orders, device_rank * modes_dev, modes_dev, 0)
    cycle_index = device_rank * cycle_rows + jnp.arange(cycle_rows, dtype=jnp.int32)
    legendre = legendre_rows(order_index, NLAT, LMAX).astype(jnp.bfloat16)
    forward, inverse = fourier_tables(NLON, all_orders)
    weighting = quad_weights(cycle_index, NLAT) * (2.0 * math.pi / NLON)
    normed = layer_norm(grid_values, spectral_gain[0]).astype(jnp.bfloat16)
    spectral = jnp.einsum("nrm,acn->marc", forward, normed, preferred_element_type=jnp.float32)
    spectral = (
        (spectral * weighting[None, :, None, None])
        .astype(jnp.bfloat16)
        .reshape(MMAX, cycle_rows, 2 * C)
    )
    coeffs = jnp.einsum(
        "mla,mak->mlk",
        legendre,
        lax.all_to_all(spectral, "sp", split_axis=0, concat_axis=1, tiled=True),
        preferred_element_type=jnp.float32,
    ).astype(jnp.bfloat16)
    half = LMAX // sp_count // 2
    plan, slots = triangle_plan(sp_count, half)
    own_weight = spectral_weight[0]
    partner = [(i, sp_count - 1 - i) for i in range(sp_count)]
    other_weight = lax.ppermute(own_weight[half:], "sp", partner)
    is_low = device_rank < sp_count // 2
    low_weight = mixing_matrix(jnp.where(is_low, own_weight[:half], other_weight))
    high_weight = mixing_matrix(jnp.where(is_low, other_weight, own_weight[:half]))
    width = coeffs.shape[2]
    pieces = []
    for low_start, low_count, high_start, high_count in plan:
        pieces.append(coeffs[:low_count, low_start : low_start + half])
        gap = slots - low_count - high_count
        if gap:
            pieces.append(jnp.zeros((gap, half, width), coeffs.dtype))
        pieces.append(coeffs[:high_count, high_start : high_start + half])
    packed = jnp.concatenate(pieces, axis=0)
    by_degree = lax.all_to_all(packed, "sp", split_axis=0, concat_axis=0, tiled=True)
    by_degree = by_degree.reshape(sp_count, slots, half, width)
    most_low = max((entry[1] for entry in plan))
    most_high = max((entry[3] for entry in plan))
    low_mixed = jnp.einsum(
        "dslk,lkj->dslj", by_degree[:, :most_low], low_weight, preferred_element_type=jnp.float32
    ).astype(jnp.bfloat16)
    high_mixed = jnp.einsum(
        "dslk,lkj->dslj",
        by_degree[:, slots - most_high :],
        high_weight,
        preferred_element_type=jnp.float32,
    ).astype(jnp.bfloat16)
    low_rows = jnp.array([entry[1] for entry in plan], jnp.int32)[device_rank]
    row = jnp.arange(slots, dtype=jnp.int32)[None, :, None, None]
    mixed = jnp.where(
        row < low_rows,
        jnp.pad(low_mixed, ((0, 0), (0, slots - most_low), (0, 0), (0, 0))),
        jnp.pad(high_mixed, ((0, 0), (slots - most_high, 0), (0, 0), (0, 0))),
    )
    returned = lax.all_to_all(
        mixed.reshape(sp_count * slots, half, width), "sp", split_axis=0, concat_axis=0, tiled=True
    ).reshape(sp_count, slots, half, width)
    parts = {}
    for rank, (low_start, low_count, high_start, high_count) in enumerate(plan):
        parts[low_start] = (returned[rank, :low_count], low_count)
        parts[high_start] = (returned[rank, slots - high_count :], high_count)
    mixed_coeffs = jnp.concatenate(
        [
            jnp.pad(parts[start][0], ((0, modes_dev - parts[start][1]), (0, 0), (0, 0)))
            for start in sorted(parts)
        ],
        axis=1,
    )
    grid_part = jnp.einsum(
        "mla,mlk->mak", legendre, mixed_coeffs, preferred_element_type=jnp.float32
    ).astype(jnp.bfloat16)
    grid_part = grid_part.reshape(modes_dev, sp_count, cycle_rows, width)
    chunk = cycle_rows // CHUNKS
    outputs = []
    for start in range(0, cycle_rows, chunk):
        on_grid = lax.all_to_all(
            grid_part[:, :, start : start + chunk].reshape(modes_dev, sp_count * chunk, width),
            "sp",
            split_axis=1,
            concat_axis=0,
            tiled=True,
        )
        synthesis = jnp.einsum(
            "marc,rmn->acn",
            on_grid.reshape(MMAX, chunk, 2, C),
            inverse,
            preferred_element_type=jnp.float32,
        )
        residual = grid_values[start : start + chunk].astype(jnp.float32) + synthesis
        hidden_in = layer_norm(residual, mixer_gain[0]).astype(jnp.bfloat16)
        hidden = jnp.einsum(
            "acn,ch->anh", hidden_in, up_weight[0], preferred_element_type=jnp.float32
        ) + up_bias[0].astype(jnp.float32)
        hidden = jax.nn.gelu(hidden, approximate=False).astype(jnp.bfloat16)
        branch = jnp.einsum(
            "anh,ch->acn", hidden, down_weight[0], preferred_element_type=jnp.float32
        )
        result = (residual + branch).astype(jnp.bfloat16)
        outputs.append(passed_along(result, "section", 1))
    return jnp.concatenate(outputs, axis=0)[None]


def solution(mesh):
    in_specs = (
        P("section", "sp", None, None),
        P("section", None),
        P("section", "sp", None, None),
        P("section", None),
        P("section", None, None),
        P("section", None),
        P("section", None, None),
    )
    out_specs = P("section", "sp", None, None)
    return jax.shard_map(shards, mesh=mesh, in_specs=in_specs, out_specs=out_specs, check_vma=False)
```

profile of v0, /device:TPU:0, one launch (start us, length us, event | category | flops | bytes accessed | tf_op | source)
XLA Modules:
  0.0 1701.2 jit_solution(16613426593756830060)
XLA Ops:
  1.2 7.8 convert_reduce_fusion
  9.0 10.3 fusion.183
  24.8 19.0 %multiply_convert_fusion = bf16[48,192,2,384]{3,1,2,0:T(8,128)(2,1)} fusion(f32[48]{0:T(128)S(1)} %subtract_multiply_fusion, bf16[1,48,192,768]{3,2,1,0:T(8,128)(2,1)} %param.14, f32[192]{0:T(256)S(1)} %bitcast.620, f32[48,768]{1,0:T(8,128)S(1)} %add_rsqrt_fusion, f32[48,768]{1,0:T(8,128)S(1)} %broadcast_multiply_fusion, ...), kind=kOutput, calls=%fused_computation.485 | convolution fusion | flops 10923540480 | bytes 29787072 | tf_op jit(solution)/shard_map/nrm,acn->marc/dot_general | solution.py:201
  43.8 18.6 %copy.34 = bf16[384,48,384]{2,1,0:T(8,128)(2,1)} copy(bf16[384,48,384]{0,2,1:T(8,128)(2,1)} %bitcast.601) | data formatting | bytes 28311552 | tf_op jit(solution)/shard_map/reshape | solution.py:205
  62.4 7.3 all-to-all-start
  72.0 59.7 %while.70 = (s32[]{:T(128)}, f32[24,48,384]{2,1,0:T(8,128)}, f32[24,48,384]{2,1,0:T(8,128)}, f32[24,48,384]{2,1,0:T(8,128)}, f32[24,48,384]{2,1,0:T(8,128)}, /*i...) while((s32[]{:T(128)}, f32[24,48,384]{2,1,0:T(8,128)}, ...), condition=%wide.region_2.3_spmd.clone.clone, body=%wide.region_1.2_spmd.clone.clone.sunk | while | flops 123129520 | bytes 200388496 | solution.py:107
  132.4 58.0 %while.69 = (s32[]{:T(128)}, f32[48,384]{1,0:T(8,128)S(1)}, f32[48,384]{1,0:T(8,128)S(1)}, f32[48,384]{1,0:T(8,128)S(1)}, f32[24,48,384]{2,1,0:T(8,128)}, /*inde...) while((s32[]{:T(128)}, f32[48,384]{1,0:T(8,128)S(1)}, ...), condition=%wide.region_4.5_spmd.clone, body=%wide.region_3.4_spmd.clone.sunk | while | flops 368643 | bytes 1548453 | solution.py:123
  190.5 100.2 %while.68 = (s32[]{:T(128)}, f32[24,48,384]{2,1,0:T(8,128)}, f32[24,48,384]{2,1,0:T(8,128)}, f32[24,48,384]{2,1,0:T(8,128)S(1)}, bf16[2,8,24,48,384]{4,1,0,2,3:T...) while((s32[]{:T(128)}, f32[24,48,384]{2,1,0:T(8,128)}, ...), condition=%wide.region_6.7_spmd.clone.clone, body=%wide.region_5.6_spmd.clone.clone.sunk | while | flops 100568752 | bytes 101660528 | solution.py:140
  211.3 7.1 bitcast_dynamic-update-slice_fusion.25
  220.7 7.1 bitcast_dynamic-update-slice_fusion.27
  233.5 7.2 copy_dynamic-update-slice_fusion.2
  261.3 7.1 bitcast_dynamic-update-slice_fusion.25
  270.7 7.1 bitcast_dynamic-update-slice_fusion.27
  283.5 7.2 copy_dynamic-update-slice_fusion.2
  290.7 14.3 fusion.186
  305.0 71.5 %all-to-all-done = bf16[384,48,384]{2,1,0:T(8,128)(2,1)} async-done(((bf16[384,48,384]{2,1,0:T(8,128)(2,1)}), bf16[384,48,384]{2,1,0:T(8,128)(2,1)}, u32[]{:S(2)}, u32[]{:S(2)}) %all-to-all-start) | async-done | bytes 14155808 | tf_op jit(solution)/shard_map/all_to_all | solution.py:210
  376.5 12.9 copy.35
  389.4 19.7 %convolution_convert_fusion.1 = bf16[48,384,384]{2,1,0:T(8,128)(2,1)} fusion(bf16[48,384,384]{2,1,0:T(8,128)(2,1)} %fusion.186, bf16[48,384,384]{2,1,0:T(8,128)(2,1)} %bitcast.579), kind=kOutput, calls=%fused_computation.578 | convolution fusion | flops 5442895872 | bytes 42467328 | tf_op jit(solution)/shard_map/mla,mak->mlk/dot_general | solution.py:207
  453.3 191.3 %collective-permute-done = bf16[24,192,384]{2,1,0:T(8,128)(2,1)} collective-permute-done((bf16[24,192,384]{2,1,0:T(8,128)(2,1)}, bf16[24,192,384]{2,1,0:T(8,128)(2,1)}, u32[]{:S(2)}, u32[]{:S(2)}) %collective-permute-start) | collective-permute-done | bytes 3538976 | tf_op jit(solution)/shard_map/ppermute | solution.py:217
  655.4 29.7 %all-to-all-done.1 = bf16[408,24,384]{2,1,0:T(8,128)(2,1)} async-done(((bf16[408,24,384]{2,1,0:T(8,128)(2,1)}), bf16[408,24,384]{2,1,0:T(8,128)(2,1)}, u32[]{:S(2)}, u32[]{:S(2)}) %all-to-all-start.1) | async-done | bytes 7520288 | tf_op jit(solution)/shard_map/all_to_all | solution.py:230
  697.1 15.2 fusion.237
  712.3 8.9 convert_bitcast_fusion.1
  731.8 12.0 pad_select_fusion
  743.8 7.9 copy.38
  751.7 252.8 %all_to_all.88 = bf16[408,24,384]{2,1,0:T(8,128)(2,1)S(1)} all-to-all(bf16[408,24,384]{2,1,0:T(8,128)(2,1)S(1)} %bitcast.596), channel_id=1, replica_groups=mesh['section'=4,'sp'=8] {'sp'}, dimensions={0} | all-to-all | bytes 15040512 | tf_op jit(solution)/shard_map/all_to_all | solution.py:250
  1021.1 19.2 %convolution_convert_fusion = bf16[48,384,384]{2,1,0:T(8,128)(2,1)} fusion(bf16[48,384,384]{2,1,0:T(8,128)(2,1)} %fusion.186, bf16[48,384,384]{2,1,0:T(8,128)(2,1)} %fusion.307), kind=kOutput, calls=%fused_computation.577 | convolution fusion | flops 5442895872 | bytes 42467328 | tf_op jit(solution)/shard_map/mla,mlk->mak/dot_general | solution.py:264
  1040.3 14.2 fusion.482
  1069.2 72.0 %all-to-all-done.5 = bf16[48,96,384]{2,0,1:T(8,128)(2,1)} async-done(((bf16[48,96,384]{2,0,1:T(8,128)(2,1)}), bf16[48,96,384]{2,0,1:T(8,128)(2,1)}, u32[]{:S(2)}, u32[]{:S(2)}) %all-to-all-start.5) | async-done | bytes 3538976 | tf_op jit(solution)/shard_map/all_to_all | solution.py:271
  1152.4 71.9 %all-to-all-done.3 = bf16[48,96,384]{2,0,1:T(8,128)(2,1)} async-done(((bf16[48,96,384]{2,0,1:T(8,128)(2,1)}), bf16[48,96,384]{2,0,1:T(8,128)(2,1)}, u32[]{:S(2)}, u32[]{:S(2)}) %all-to-all-start.3) | async-done | bytes 3538976 | tf_op jit(solution)/shard_map/all_to_all | solution.py:271
  1235.0 72.4 %all-to-all-done.6 = bf16[48,96,384]{2,0,1:T(8,128)(2,1)} async-done(((bf16[48,96,384]{2,0,1:T(8,128)(2,1)}), bf16[48,96,384]{2,0,1:T(8,128)(2,1)}, u32[]{:S(2)}, u32[]{:S(2)}) %all-to-all-start.6) | async-done | bytes 3538976 | tf_op jit(solution)/shard_map/all_to_all | solution.py:271
  1317.6 9.5 copy.61
  1327.2 12.9 reshape.7129
  1340.1 9.5 copy.58
  1349.7 13.0 reshape.7126
  1362.6 9.5 copy.60
  1372.1 13.1 reshape.7128
  1413.7 9.5 copy.59
  1423.2 13.1 reshape.7127
  1446.2 6.9 fusion.264
  1459.6 6.9 fusion.266
  1466.4 32.9 %fusion.251 = (u16[768,384]{1,0:T(8,128)(2,1)S(1)}, u16[768,384]{1,0:T(8,128)(2,1)S(1)}, u16[768,384]{1,0:T(8,128)(2,1)S(1)}, u16[768,384]{1,0:T(8,128)(2,1)S(1)...) fusion(f32[384]{0:T(512)S(1)} %convert_reduce_fusion.1, ...), kind=kOutput, calls=%fused_computation.617 | convolution fusion | flops 1561853952 | bytes 68643072 | tf_op jit(solution)/shard_map/acn,ch->anh/dot_general | solution.py:286
  1499.3 37.1 %fusion.246 = bf16[12,192,768]{2,1,0:T(8,128)(2,1)} fusion(f32[12,192,768]{2,1,0:T(8,128)} %copy-done.21, f32[12,768,384]{2,1,0:T(8,128)} %get-tuple-element.1155, f32[384]{0:T(512)S(1)} %convert_reduce_fusion.1, u16[768,384]{1,0:T(8,128)(2,1)S(1)} %get-tuple-element.775, u16[768,384]{1,0:T(8,128)(2,1)S(1)} %get-tuple-element.774, ...), kind=kOutput, calls=%fused_computation.603 | convolution fusion | flops 1613758464 | bytes 26101248 | tf_op jit(solution)/shard_map/anh,ch->acn/dot_general | solution.py:290
  1536.5 37.0 %fusion.243 = bf16[12,192,768]{2,1,0:T(8,128)(2,1)} fusion(f32[12,192,768]{2,1,0:T(8,128)} %copy-done.8, f32[12,768,384]{2,1,0:T(8,128)S(1)} %copy-done.18, f32[384]{0:T(512)S(1)} %convert_reduce_fusion.1, u16[768,384]{1,0:T(8,128)(2,1)S(1)} %get-tuple-element.782, u16[768,384]{1,0:T(8,128)(2,1)S(1)} %get-tuple-element.783, ...), kind=kOutput, calls=%fused_computation.597 | convolution fusion | flops 1613758464 | bytes 26101248 | tf_op jit(solution)/shard_map/anh,ch->acn/dot_general | solution.py:290
  1575.0 36.2 %fusion.244 = bf16[12,192,768]{2,1,0:T(8,128)(2,1)} fusion(f32[12,192,768]{2,1,0:T(8,128)S(1)} %copy-done.10, f32[12,768,384]{2,1,0:T(8,128)S(1)} %copy-done.17, f32[384]{0:T(512)S(1)} %convert_reduce_fusion.1, u16[768,384]{1,0:T(8,128)(2,1)} %get-tuple-element.784, u16[768,384]{1,0:T(8,128)(2,1)} %get-tuple-element.785, ...), kind=kOutput, calls=%fused_computation.599 | convolution fusion | flops 1613758464 | bytes 26101248 | tf_op jit(solution)/shard_map/anh,ch->acn/dot_general | solution.py:290
  1611.3 33.9 %fusion.245 = bf16[12,192,768]{2,1,0:T(8,128)(2,1)S(1)} fusion(f32[12,192,768]{2,1,0:T(8,128)S(1)} %copy-done.12, f32[12,768,384]{2,1,0:T(8,128)S(1)} %copy-done.16, f32[384]{0:T(512)S(1)} %convert_reduce_fusion.1, u16[768,384]{1,0:T(8,128)(2,1)S(1)} %copy-done.34, u16[768,384]{1,0:T(8,128)(2,1)S(1)} %copy-done.35, bf16[1,192,384]{2,1,0:T(8,128)(2,1)S(1)} %copy-done.32), kind=kOutput, calls=%fused_computation.601 | convolution fusion | flops 1613758464 | bytes 26101248 | tf_op jit(solution)/shard_map/anh,ch->acn/dot_general | solution.py:290
  1645.9 7.5 collective-permute-done.3
  1653.4 37.9 %collective-permute-done.2 = bf16[12,192,768]{2,1,0:T(8,128)(2,1)S(1)} collective-permute-done((bf16[12,192,768]{2,1,0:T(8,128)(2,1)S(1)}, bf16[12,192,768]{2,1,0:T(8,128)(2,1)S(1)}, u32[]{:S(2)}, u32[]{:S(2)}) %collective-permute-start.2) | collective-permute-done | bytes 3538976 | tf_op jit(solution)/shard_map/ppermute | solution.py:18
  1691.3 9.6 maximum_bitcast_fusion
  (454 shorter events, 369.5 us)
Async XLA Ops:
  0.0 1446.2 %copy-start = (bf16[1,192,384]{2,1,0:T(8,128)(2,1)S(1)}, bf16[1,192,384]{2,1,0:T(8,128)(2,1)}, u32[]{:S(2)}) copy-start(bf16[1,192,384]{2,1,0:T(8,128)(2,1)} %param.18) | copy-start | bytes 442372
  0.0 70.3 %copy-start.25 = (s32[384]{0:T(512)}, s32[384]{0:T(512)S(1)}, u32[]{:S(2)}) copy-start(s32[384]{0:T(512)S(1)} %fusion.328) | copy-start | bytes 4612
  62.4 314.1 %all-to-all-start = ((bf16[384,48,384]{2,1,0:T(8,128)(2,1)}), bf16[384,48,384]{2,1,0:T(8,128)(2,1)}, u32[]{:S(2)}, u32[]{:S(2)}) async-start(bf16[384,48,384]{2,1,0:T(8,128)(2,1)} %copy.34), calls=%async_computation | async-start | bytes 28311552 | tf_op jit(solution)/shard_map/all_to_all | solution.py:210
  71.9 59.7 %copy-start.27 = (f32[384]{0:T(512)S(1)}, f32[384]{0:T(512)}, u32[]{:S(2)}) copy-start(f32[384]{0:T(512)} %sine_log_fusion) | copy-start | bytes 4612
  71.9 59.7 %copy-start.31 = (f32[48]{0:T(128)S(1)}, f32[48]{0:T(128)}, u32[]{:S(2)}) copy-start(f32[48]{0:T(128)} %add_multiply_fusion.16) | copy-start | bytes 580
  71.9 60.4 %copy-start.1 = (f32[24,48,384]{2,1,0:T(8,128)S(1)}, f32[24,48,384]{2,1,0:T(8,128)}, u32[]{:S(2)}) copy-start(f32[24,48,384]{2,1,0:T(8,128)} %custom-call.13) | copy-start | bytes 5308420
  71.9 60.4 %copy-start.19 = (f32[48,384]{1,0:T(8,128)S(1)}, f32[48,384]{1,0:T(8,128)}, u32[]{:S(2)}) copy-start(f32[48,384]{1,0:T(8,128)} %custom-call) | copy-start | bytes 221188
  72.0 60.4 %copy-start.20 = (f32[48,384]{1,0:T(8,128)S(1)}, f32[48,384]{1,0:T(8,128)}, u32[]{:S(2)}) copy-start(f32[48,384]{1,0:T(8,128)} %custom-call.1) | copy-start | bytes 221188
  87.6 4.4 copy-start.6
  96.6 3.9 copy-start.7
  101.5 5.5 copy-start.2
  101.5 5.5 copy-start.3
  101.5 5.5 copy-start.4
  101.5 5.5 copy-start.5
  118.6 4.4 copy-start.6
  127.7 3.9 copy-start.7
  190.4 100.2 %copy-start.24 = (pred[48,384]{1,0:T(8,128)(4,1)S(1)}, pred[48,384]{1,0:T(8,128)(4,1)}, u32[]{:S(2)}) copy-start(pred[48,384]{1,0:T(8,128)(4,1)} %iota_compare_fusion) | copy-start | bytes 55300
  438.5 246.6 %all-to-all-start.1 = ((bf16[408,24,384]{2,1,0:T(8,128)(2,1)}), bf16[408,24,384]{2,1,0:T(8,128)(2,1)}, u32[]{:S(2)}, u32[]{:S(2)}) async-start(bf16[408,24,384]{2,1,0:T(8,128)(2,1)} %slice_dynamic-update-slice_fusion.1), calls=%async_computation.1 | async-start | bytes 15040512 | tf_op jit(solution)/shard_map/all_to_all | solution.py:230
  443.4 8.8 copy-start.33
  447.5 197.0 %collective-permute-start = (bf16[24,192,384]{2,1,0:T(8,128)(2,1)}, bf16[24,192,384]{2,1,0:T(8,128)(2,1)}, u32[]{:S(2)}, u32[]{:S(2)}) collective-permute-start(bf16[24,192,384]{2,1,0:T(8,128)(2,1)} %slice_bitcast_fusion), channel_id=1, source_target_pairs={{0,7},{1,6},{2,5},{3,4},{4,3},{5,2},{6,1},{7,0},{8,15},{9,14},{10,... | collective-permute-start | bytes 10616840 | tf_op jit(solution)/shard_map/ppermute | solution.py:217
  1058.4 82.8 %all-to-all-start.5 = ((bf16[48,96,384]{2,0,1:T(8,128)(2,1)}), bf16[48,96,384]{2,0,1:T(8,128)(2,1)}, u32[]{:S(2)}, u32[]{:S(2)}) async-start(bf16[48,96,384]{2,0,1:T(8,128)(2,1)} %bitcast.605), calls=%async_computation.5 | async-start | bytes 7077888 | tf_op jit(solution)/shard_map/all_to_all | solution.py:271
  1141.2 83.0 %all-to-all-start.3 = ((bf16[48,96,384]{2,0,1:T(8,128)(2,1)}), bf16[48,96,384]{2,0,1:T(8,128)(2,1)}, u32[]{:S(2)}, u32[]{:S(2)}) async-start(bf16[48,96,384]{2,0,1:T(8,128)(2,1)} %bitcast.604), calls=%async_computation.3 | async-start | bytes 7077888 | tf_op jit(solution)/shard_map/all_to_all | solution.py:271
  1224.2 83.1 %all-to-all-start.6 = ((bf16[48,96,384]{2,0,1:T(8,128)(2,1)}), bf16[48,96,384]{2,0,1:T(8,128)(2,1)}, u32[]{:S(2)}, u32[]{:S(2)}) async-start(bf16[48,96,384]{2,0,1:T(8,128)(2,1)} %bitcast.603), calls=%async_computation.6 | async-start | bytes 7077888 | tf_op jit(solution)/shard_map/all_to_all | solution.py:271
  1307.4 4.7 copy-start.30
  1307.4 4.7 copy-start.29
  1307.4 4.7 copy-start.26
  1307.4 106.3 %all-to-all-start.4 = ((bf16[48,96,384]{2,0,1:T(8,128)(2,1)}), bf16[48,96,384]{2,0,1:T(8,128)(2,1)}, u32[]{:S(2)}, u32[]{:S(2)}) async-start(bf16[48,96,384]{2,0,1:T(8,128)(2,1)} %bitcast.602), calls=%async_computation.4 | async-start | bytes 7077888 | tf_op jit(solution)/shard_map/all_to_all | solution.py:271
  1391.5 3.6 copy-start.8
  1391.5 4.6 copy-start.23
  1401.2 3.6 copy-start.21
  1401.2 4.6 copy-start.22
  1442.6 3.6 copy-start.11
  1442.6 10.4 slice-start.2
  1446.2 6.9 slice-start.3
  1446.2 13.4 slice-start
  1453.0 6.5 slice-start.1
  1466.4 32.9 %copy-start.32 = (bf16[1,192,384]{2,1,0:T(8,128)(2,1)S(1)}, bf16[1,192,384]{2,1,0:T(8,128)(2,1)}, u32[]{:S(2)}) copy-start(bf16[1,192,384]{2,1,0:T(8,128)(2,1)} %param.20) | copy-start | bytes 442372
  1499.3 37.1 %copy-start.18 = (f32[12,768,384]{2,1,0:T(8,128)S(1)}, f32[12,768,384]{2,1,0:T(8,128)}, u32[]{:S(2)}) copy-start(f32[12,768,384]{2,1,0:T(8,128)} %fusion.266) | copy-start | bytes 42467332
  1536.4 109.5 %collective-permute-start.1 = (bf16[12,192,768]{2,1,0:T(8,128)(2,1)}, bf16[12,192,768]{2,1,0:T(8,128)(2,1)}, u32[]{:S(2)}, u32[]{:S(2)}) collective-permute-start(bf16[12,192,768]{2,1,0:T(8,128)(2,1)} %fusion.246), channel_id=1, source_target_pairs={{0,8},{8,16},{16,24},{24,0},{1,9},{9,17},{17,25},{25,1},{2,10},{10... | collective-permute-start | bytes 10616840 | tf_op jit(solution)/shard_map/ppermute | solution.py:18
  1536.4 38.6 %copy-start.10 = (f32[12,192,768]{2,1,0:T(8,128)S(1)}, f32[12,192,768]{2,1,0:T(8,128)}, u32[]{:S(2)}) copy-start(f32[12,192,768]{2,1,0:T(8,128)} %copy-done.9) | copy-start | bytes 21233668
  1536.4 38.6 %copy-start.17 = (f32[12,768,384]{2,1,0:T(8,128)S(1)}, f32[12,768,384]{2,1,0:T(8,128)}, u32[]{:S(2)}) copy-start(f32[12,768,384]{2,1,0:T(8,128)} %fusion.265) | copy-start | bytes 42467332
  1573.4 72.5 %collective-permute-start.4 = (bf16[12,192,768]{2,1,0:T(8,128)(2,1)}, bf16[12,192,768]{2,1,0:T(8,128)(2,1)}, u32[]{:S(2)}, u32[]{:S(2)}) collective-permute-start(bf16[12,192,768]{2,1,0:T(8,128)(2,1)} %fusion.243), channel_id=1, source_target_pairs={{0,8},{8,16},{16,24},{24,0},{1,9},{9,17},{17,25},{25,1},{2,10},{10... | collective-permute-start | bytes 10616840 | tf_op jit(solution)/shard_map/ppermute | solution.py:18
  1575.0 36.3 %copy-start.12 = (f32[12,192,768]{2,1,0:T(8,128)S(1)}, f32[12,192,768]{2,1,0:T(8,128)}, u32[]{:S(2)}) copy-start(f32[12,192,768]{2,1,0:T(8,128)} %copy-done.11) | copy-start | bytes 21233668
  1575.0 36.3 %copy-start.16 = (f32[12,768,384]{2,1,0:T(8,128)S(1)}, f32[12,768,384]{2,1,0:T(8,128)}, u32[]{:S(2)}) copy-start(f32[12,768,384]{2,1,0:T(8,128)} %fusion.264) | copy-start | bytes 42467332
  1575.0 36.3 %copy-start.34 = (u16[768,384]{1,0:T(8,128)(2,1)S(1)}, u16[768,384]{1,0:T(8,128)(2,1)}, u32[]{:S(2)}) copy-start(u16[768,384]{1,0:T(8,128)(2,1)} %get-tuple-element.786) | copy-start | bytes 1769476
  1575.0 36.3 %copy-start.35 = (u16[768,384]{1,0:T(8,128)(2,1)S(1)}, u16[768,384]{1,0:T(8,128)(2,1)}, u32[]{:S(2)}) copy-start(u16[768,384]{1,0:T(8,128)(2,1)} %get-tuple-element.787) | copy-start | bytes 1769476
  1611.3 42.1 %collective-permute-start.3 = (bf16[12,192,768]{2,1,0:T(8,128)(2,1)}, bf16[12,192,768]{2,1,0:T(8,128)(2,1)S(1)}, u32[]{:S(2)}, u32[]{:S(2)}) collective-permute-start(bf16[12,192,768]{2,1,0:T(8,128)(2,1)} %fusion.244), channel_id=1, source_target_pairs={{0,8},{8,16},{16,24},{24,0},{1,9},{9,17},{17,25},{25,1},{2,10},{10... | collective-permute-start | bytes 10616840 | tf_op jit(solution)/shard_map/ppermute | solution.py:18
  1645.2 46.1 %collective-permute-start.2 = (bf16[12,192,768]{2,1,0:T(8,128)(2,1)S(1)}, bf16[12,192,768]{2,1,0:T(8,128)(2,1)S(1)}, u32[]{:S(2)}, u32[]{:S(2)}) collective-permute-start(bf16[12,192,768]{2,1,0:T(8,128)(2,1)S(1)} %fusion.245), channel_id=1, source_target_pairs={{0,8},{8,16},{16,24},{24,0},{1,9},{9,17},{17,25},{25,1},{2,10},{10... | collective-permute-start | bytes 10616840 | tf_op jit(solution)/shard_map/ppermute | solution.py:18
  (9 other events, 21.8 us)
where the time goes:
time: 1710 us; the launch traced here: 1700 us
  waiting for transfers between devices  554 us (32%)
  matrix products  298 us (17%)
  other arithmetic  291 us (17%)
  local copies, waits for them, and re-layouts  264 us (15%)
  blocking collectives  253 us (15%)
  starting transfers between devices  37.7 us (2%)
    all_to_all x1, blocking collectives, shards(): lax.all_to_all(mixed.reshape(sp_count * slots, half, width), 'sp', split_...  253 us
    all_to_all x4, waiting for transfers between devices, shards(): lax.all_to_all(grid_part[:, :, start:start + chunk].reshape(modes_dev, sp...  216 us
    ppermute x1, waiting for transfers between devices, shards(): other_weight = lax.ppermute(own_weight[half:], 'sp', partner)  191 us
    dot_general x4, matrix products, shards(): jnp.einsum('anh,ch->acn', hidden, down_weight[0], preferred_element_type=...  144 us
    reshape x8, local copies, waits for them, and re-layouts, shards(): on_grid.reshape(MMAX, chunk, 2, C)  90.3 us
    unnamed x104, local copies, waits for them, and re-layouts  87.1 us
    all_to_all x1, waiting for transfers between devices, shards(): lax.all_to_all(spectral, 'sp', split_axis=0, concat_axis=1, tiled=True)  71.5 us
    while x14, other arithmetic  69.9 us
  transfers between devices with their start and end apart: 11, of which 8 were waited for; matrix products, arithmetic and copies ran while one was open for 27% of the time, Pallas kernels for 0%

commit v1 on v0

--- a/solution.py
+++ b/solution.py
@@ -268,12 +268,22 @@
     chunk = cycle_rows // CHUNKS
     outputs = []
     for start in range(0, cycle_rows, chunk):
-        on_grid = lax.all_to_all(
-            grid_part[:, :, start : start + chunk].reshape(modes_dev, sp_count * chunk, width),
-            "sp",
-            split_axis=1,
-            concat_axis=0,
-            tiled=True,
+        on_grid = jnp.concatenate(
+            lax.all_to_all(
+                jnp.stack(
+                    jnp.split(
+                        grid_part[:, :, start : start + chunk].reshape(
+                            modes_dev, sp_count * chunk, width
+                        ),
+                        lax.axis_size("sp"),
+                        axis=1,
+                    )
+                ),
+                "sp",
+                0,
+                0,
+            ),
+            axis=0,
         )
         synthesis = jnp.einsum(
             "marc,rmn->acn",

time: 1710 us -> 1720 us (level)
  local copies, waits for them, and re-layouts: 264 us -> 283 us
    another operation x0 -> x12, local copies, waits for them, and re-layouts: none -> 93.5 us  [the longest x8 90.3 us: shards(): on_grid.reshape(MMAX, chunk, 2, C)]
    reshape x8 -> x0, local copies, waits for them, and re-layouts: 90.3 us -> none  [shards(): on_grid.reshape(MMAX, chunk, 2, C)]
    unnamed x104 -> x132, local copies, waits for them, and re-layouts: 87.1 us -> 103 us
  transfers between devices with their start and end apart: 11 -> 11, of which waited for: 8 -> 8; matrix products, arithmetic and copies ran while one was open for 27% -> 28% of each run, Pallas kernels for 0% -> 0%
where the time goes in v1:
time: 1720 us; the launch traced here: 1710 us
  waiting for transfers between devices  540 us (31%)
  matrix products  298 us (17%)
  other arithmetic  291 us (17%)
  local copies, waits for them, and re-layouts  283 us (16%)
  blocking collectives  253 us (15%)
  starting transfers between devices  37.6 us (2%)
    all_to_all x1, blocking collectives, shards(): lax.all_to_all(mixed.reshape(sp_count * slots, half, width), 'sp', split_...  253 us
    all_to_all x4, waiting for transfers between devices, shards(): lax.all_to_all(jnp.stack(jnp.split(grid_part[:, :, start:start + chunk].r...  202 us
    ppermute x1, waiting for transfers between devices, shards(): other_weight = lax.ppermute(own_weight[half:], 'sp', partner)  191 us
    dot_general x4, matrix products, shards(): jnp.einsum('anh,ch->acn', hidden, down_weight[0], preferred_element_type=...  144 us
    unnamed x132, local copies, waits for them, and re-layouts  103 us
    another operation x8, local copies, waits for them, and re-layouts, shards(): on_grid.reshape(MMAX, chunk, 2, C)  90.3 us
    all_to_all x1, waiting for transfers between devices, shards(): lax.all_to_all(spectral, 'sp', split_axis=0, concat_axis=1, tiled=True)  71.5 us
    while x14, other arithmetic  69.9 us
  transfers between devices with their start and end apart: 11, of which 8 were waited for; matrix products, arithmetic and copies ran while one was open for 28% of the time, Pallas kernels for 0%

profile of v1, /device:TPU:0, one launch (start us, length us, event | category | flops | bytes accessed | tf_op | source)
XLA Modules:
  0.0 1706.1 jit_solution(10296813555082019848)
XLA Ops:
  1.2 7.8 convert_reduce_fusion
  9.0 10.3 fusion.183
  24.8 19.0 %multiply_convert_fusion = bf16[48,192,2,384]{3,1,2,0:T(8,128)(2,1)} fusion(f32[48]{0:T(128)S(1)} %subtract_multiply_fusion, bf16[1,48,192,768]{3,2,1,0:T(8,128)(2,1)} %param.14, f32[192]{0:T(256)S(1)} %bitcast.764, f32[48,768]{1,0:T(8,128)S(1)} %add_rsqrt_fusion, f32[48,768]{1,0:T(8,128)S(1)} %broadcast_multiply_fusion, ...), kind=kOutput, calls=%fused_computation.485 | convolution fusion | flops 10923540480 | bytes 29787072 | tf_op jit(solution)/shard_map/nrm,acn->marc/dot_general | solution.py:201
  43.8 18.6 %copy.66 = bf16[384,48,384]{2,1,0:T(8,128)(2,1)} copy(bf16[384,48,384]{0,2,1:T(8,128)(2,1)} %bitcast.717) | data formatting | bytes 28311552 | tf_op jit(solution)/shard_map/reshape | solution.py:205
  62.4 7.3 all-to-all-start
  72.0 59.7 %while.70 = (s32[]{:T(128)}, f32[24,48,384]{2,1,0:T(8,128)}, f32[24,48,384]{2,1,0:T(8,128)}, f32[24,48,384]{2,1,0:T(8,128)}, f32[24,48,384]{2,1,0:T(8,128)}, /*i...) while((s32[]{:T(128)}, f32[24,48,384]{2,1,0:T(8,128)}, ...), condition=%wide.region_2.3_spmd.clone.clone, body=%wide.region_1.2_spmd.clone.clone.sunk | while | flops 123129520 | bytes 200388496 | solution.py:107
  132.4 58.0 %while.69 = (s32[]{:T(128)}, f32[48,384]{1,0:T(8,128)S(1)}, f32[48,384]{1,0:T(8,128)S(1)}, f32[48,384]{1,0:T(8,128)S(1)}, f32[24,48,384]{2,1,0:T(8,128)}, /*inde...) while((s32[]{:T(128)}, f32[48,384]{1,0:T(8,128)S(1)}, ...), condition=%wide.region_4.5_spmd.clone, body=%wide.region_3.4_spmd.clone.sunk | while | flops 368643 | bytes 1548453 | solution.py:123
  190.5 100.2 %while.68 = (s32[]{:T(128)}, f32[24,48,384]{2,1,0:T(8,128)}, f32[24,48,384]{2,1,0:T(8,128)}, f32[24,48,384]{2,1,0:T(8,128)S(1)}, bf16[2,8,24,48,384]{4,1,0,2,3:T...) while((s32[]{:T(128)}, f32[24,48,384]{2,1,0:T(8,128)}, ...), condition=%wide.region_6.7_spmd.clone.clone, body=%wide.region_5.6_spmd.clone.clone.sunk | while | flops 100568752 | bytes 101660528 | solution.py:140
  211.3 7.1 bitcast_dynamic-update-slice_fusion.25
  220.7 7.1 bitcast_dynamic-update-slice_fusion.27
  233.5 7.2 copy_dynamic-update-slice_fusion.2
  261.3 7.1 bitcast_dynamic-update-slice_fusion.25
  270.7 7.1 bitcast_dynamic-update-slice_fusion.27
  283.5 7.2 copy_dynamic-update-slice_fusion.2
  290.7 14.3 fusion.186
  305.0 71.5 %all-to-all-done = bf16[384,48,384]{2,1,0:T(8,128)(2,1)} async-done(((bf16[384,48,384]{2,1,0:T(8,128)(2,1)}), bf16[384,48,384]{2,1,0:T(8,128)(2,1)}, u32[]{:S(2)}, u32[]{:S(2)}) %all-to-all-start) | async-done | bytes 14155808 | tf_op jit(solution)/shard_map/all_to_all | solution.py:210
  376.5 12.9 copy.67
  389.4 19.7 %convolution_convert_fusion.1 = bf16[48,384,384]{2,1,0:T(8,128)(2,1)} fusion(bf16[48,384,384]{2,1,0:T(8,128)(2,1)} %fusion.186, bf16[48,384,384]{2,1,0:T(8,128)(2,1)} %bitcast.695), kind=kOutput, calls=%fused_computation.578 | convolution fusion | flops 5442895872 | bytes 42467328 | tf_op jit(solution)/shard_map/mla,mak->mlk/dot_general | solution.py:207
  453.3 191.3 %collective-permute-done = bf16[24,192,384]{2,1,0:T(8,128)(2,1)} collective-permute-done((bf16[24,192,384]{2,1,0:T(8,128)(2,1)}, bf16[24,192,384]{2,1,0:T(8,128)(2,1)}, u32[]{:S(2)}, u32[]{:S(2)}) %collective-permute-start) | collective-permute-done | bytes 3538976 | tf_op jit(solution)/shard_map/ppermute | solution.py:217
  655.4 29.7 %all-to-all-done.1 = bf16[408,24,384]{2,1,0:T(8,128)(2,1)} async-done(((bf16[408,24,384]{2,1,0:T(8,128)(2,1)}), bf16[408,24,384]{2,1,0:T(8,128)(2,1)}, u32[]{:S(2)}, u32[]{:S(2)}) %all-to-all-start.1) | async-done | bytes 7520288 | tf_op jit(solution)/shard_map/all_to_all | solution.py:230
  697.1 15.2 fusion.237
  712.3 8.9 convert_bitcast_fusion.1
  731.8 12.0 pad_select_fusion
  743.8 7.9 copy.70
  751.7 252.8 %all_to_all.48 = bf16[408,24,384]{2,1,0:T(8,128)(2,1)S(1)} all-to-all(bf16[408,24,384]{2,1,0:T(8,128)(2,1)S(1)} %bitcast.712), channel_id=1, replica_groups=mesh['section'=4,'sp'=8] {'sp'}, dimensions={0} | all-to-all | bytes 15040512 | tf_op jit(solution)/shard_map/all_to_all | solution.py:250
  1021.1 19.2 %convolution_convert_fusion = bf16[48,384,384]{2,1,0:T(8,128)(2,1)} fusion(bf16[48,384,384]{2,1,0:T(8,128)(2,1)} %fusion.186, bf16[48,384,384]{2,1,0:T(8,128)(2,1)} %fusion.307), kind=kOutput, calls=%fused_computation.577 | convolution fusion | flops 5442895872 | bytes 42467328 | tf_op jit(solution)/shard_map/mla,mlk->mak/dot_general | solution.py:264
  1040.3 14.2 fusion.514
  1079.2 67.2 %all-to-all-done.5 = bf16[8,48,12,384]{3,1,2,0:T(8,128)(2,1)} async-done(((bf16[8,48,12,384]{3,1,2,0:T(8,128)(2,1)}), bf16[8,48,12,384]{3,1,2,0:T(8,128)(2,1)}, u32[]{:S(2)}, u32[]{:S(2)}) %all-to-all-start.5) | async-done | bytes 3538976 | tf_op jit(solution)/shard_map/all_to_all | solution.py:272
  1161.8 67.6 %all-to-all-done.3 = bf16[8,48,12,384]{3,1,2,0:T(8,128)(2,1)} async-done(((bf16[8,48,12,384]{3,1,2,0:T(8,128)(2,1)}), bf16[8,48,12,384]{3,1,2,0:T(8,128)(2,1)}, u32[]{:S(2)}, u32[]{:S(2)}) %all-to-all-start.3) | async-done | bytes 3538976 | tf_op jit(solution)/shard_map/all_to_all | solution.py:272
  1244.9 67.6 %all-to-all-done.6 = bf16[8,48,12,384]{3,1,2,0:T(8,128)(2,1)} async-done(((bf16[8,48,12,384]{3,1,2,0:T(8,128)(2,1)}), bf16[8,48,12,384]{3,1,2,0:T(8,128)(2,1)}, u32[]{:S(2)}, u32[]{:S(2)}) %all-to-all-start.6) | async-done | bytes 3538976 | tf_op jit(solution)/shard_map/all_to_all | solution.py:272
  1322.6 9.5 copy.93
  1332.1 12.9 reshape.7109
  1345.1 9.5 copy.90
  1354.6 13.0 reshape.7106
  1367.6 9.5 copy.92
  1377.1 13.1 reshape.7108
  1418.6 9.5 copy.91
  1428.2 13.1 reshape.7107
  1451.1 6.9 fusion.264
  1464.5 6.9 fusion.266
  1471.4 32.9 %fusion.251 = (u16[768,384]{1,0:T(8,128)(2,1)S(1)}, u16[768,384]{1,0:T(8,128)(2,1)S(1)}, u16[768,384]{1,0:T(8,128)(2,1)S(1)}, u16[768,384]{1,0:T(8,128)(2,1)S(1)...) fusion(f32[384]{0:T(512)S(1)} %convert_reduce_fusion.1, ...), kind=kOutput, calls=%fused_computation.617 | convolution fusion | flops 1561853952 | bytes 68643072 | tf_op jit(solution)/shard_map/acn,ch->anh/dot_general | solution.py:296
  1504.3 37.1 %fusion.246 = bf16[12,192,768]{2,1,0:T(8,128)(2,1)} fusion(f32[12,192,768]{2,1,0:T(8,128)} %copy-done.21, f32[12,768,384]{2,1,0:T(8,128)} %get-tuple-element.1155, f32[384]{0:T(512)S(1)} %convert_reduce_fusion.1, u16[768,384]{1,0:T(8,128)(2,1)S(1)} %get-tuple-element.775, u16[768,384]{1,0:T(8,128)(2,1)S(1)} %get-tuple-element.774, ...), kind=kOutput, calls=%fused_computation.603 | convolution fusion | flops 1613758464 | bytes 26101248 | tf_op jit(solution)/shard_map/anh,ch->acn/dot_general | solution.py:300
  1541.4 37.0 %fusion.243 = bf16[12,192,768]{2,1,0:T(8,128)(2,1)} fusion(f32[12,192,768]{2,1,0:T(8,128)} %copy-done.8, f32[12,768,384]{2,1,0:T(8,128)S(1)} %copy-done.18, f32[384]{0:T(512)S(1)} %convert_reduce_fusion.1, u16[768,384]{1,0:T(8,128)(2,1)S(1)} %get-tuple-element.782, u16[768,384]{1,0:T(8,128)(2,1)S(1)} %get-tuple-element.783, ...), kind=kOutput, calls=%fused_computation.597 | convolution fusion | flops 1613758464 | bytes 26101248 | tf_op jit(solution)/shard_map/anh,ch->acn/dot_general | solution.py:300
  1580.0 36.2 %fusion.244 = bf16[12,192,768]{2,1,0:T(8,128)(2,1)} fusion(f32[12,192,768]{2,1,0:T(8,128)S(1)} %copy-done.10, f32[12,768,384]{2,1,0:T(8,128)S(1)} %copy-done.17, f32[384]{0:T(512)S(1)} %convert_reduce_fusion.1, u16[768,384]{1,0:T(8,128)(2,1)} %get-tuple-element.784, u16[768,384]{1,0:T(8,128)(2,1)} %get-tuple-element.785, ...), kind=kOutput, calls=%fused_computation.599 | convolution fusion | flops 1613758464 | bytes 26101248 | tf_op jit(solution)/shard_map/anh,ch->acn/dot_general | solution.py:300
  1616.3 33.9 %fusion.245 = bf16[12,192,768]{2,1,0:T(8,128)(2,1)S(1)} fusion(f32[12,192,768]{2,1,0:T(8,128)S(1)} %copy-done.12, f32[12,768,384]{2,1,0:T(8,128)S(1)} %copy-done.16, f32[384]{0:T(512)S(1)} %convert_reduce_fusion.1, u16[768,384]{1,0:T(8,128)(2,1)S(1)} %copy-done.34, u16[768,384]{1,0:T(8,128)(2,1)S(1)} %copy-done.35, bf16[1,192,384]{2,1,0:T(8,128)(2,1)S(1)} %copy-done.32), kind=kOutput, calls=%fused_computation.601 | convolution fusion | flops 1613758464 | bytes 26101248 | tf_op jit(solution)/shard_map/anh,ch->acn/dot_general | solution.py:300
  1650.8 7.5 collective-permute-done.3
  1658.3 37.9 %collective-permute-done.2 = bf16[12,192,768]{2,1,0:T(8,128)(2,1)S(1)} collective-permute-done((bf16[12,192,768]{2,1,0:T(8,128)(2,1)S(1)}, bf16[12,192,768]{2,1,0:T(8,128)(2,1)S(1)}, u32[]{:S(2)}, u32[]{:S(2)}) %collective-permute-start.2) | collective-permute-done | bytes 3538976 | tf_op jit(solution)/shard_map/ppermute | solution.py:18
  1696.2 9.6 maximum_bitcast_fusion
  (486 shorter events, 388.3 us)
Async XLA Ops:
  0.0 1451.1 %copy-start = (bf16[1,192,384]{2,1,0:T(8,128)(2,1)S(1)}, bf16[1,192,384]{2,1,0:T(8,128)(2,1)}, u32[]{:S(2)}) copy-start(bf16[1,192,384]{2,1,0:T(8,128)(2,1)} %param.18) | copy-start | bytes 442372
  0.0 70.3 %copy-start.25 = (s32[384]{0:T(512)}, s32[384]{0:T(512)S(1)}, u32[]{:S(2)}) copy-start(s32[384]{0:T(512)S(1)} %fusion.360) | copy-start | bytes 4612
  62.4 314.1 %all-to-all-start = ((bf16[384,48,384]{2,1,0:T(8,128)(2,1)}), bf16[384,48,384]{2,1,0:T(8,128)(2,1)}, u32[]{:S(2)}, u32[]{:S(2)}) async-start(bf16[384,48,384]{2,1,0:T(8,128)(2,1)} %copy.66), calls=%async_computation | async-start | bytes 28311552 | tf_op jit(solution)/shard_map/all_to_all | solution.py:210
  71.9 59.7 %copy-start.27 = (f32[384]{0:T(512)S(1)}, f32[384]{0:T(512)}, u32[]{:S(2)}) copy-start(f32[384]{0:T(512)} %sine_log_fusion) | copy-start | bytes 4612
  71.9 59.7 %copy-start.31 = (f32[48]{0:T(128)S(1)}, f32[48]{0:T(128)}, u32[]{:S(2)}) copy-start(f32[48]{0:T(128)} %add_multiply_fusion.16) | copy-start | bytes 580
  71.9 60.4 %copy-start.1 = (f32[24,48,384]{2,1,0:T(8,128)S(1)}, f32[24,48,384]{2,1,0:T(8,128)}, u32[]{:S(2)}) copy-start(f32[24,48,384]{2,1,0:T(8,128)} %custom-call.17) | copy-start | bytes 5308420
  71.9 60.4 %copy-start.19 = (f32[48,384]{1,0:T(8,128)S(1)}, f32[48,384]{1,0:T(8,128)}, u32[]{:S(2)}) copy-start(f32[48,384]{1,0:T(8,128)} %custom-call) | copy-start | bytes 221188
  72.0 60.4 %copy-start.20 = (f32[48,384]{1,0:T(8,128)S(1)}, f32[48,384]{1,0:T(8,128)}, u32[]{:S(2)}) copy-start(f32[48,384]{1,0:T(8,128)} %custom-call.1) | copy-start | bytes 221188
  87.6 4.4 copy-start.6
  96.6 3.9 copy-start.7
  101.5 5.5 copy-start.2
  101.5 5.5 copy-start.3
  101.5 5.5 copy-start.4
  101.5 5.5 copy-start.5
  118.6 4.4 copy-start.6
  127.7 3.9 copy-start.7
  190.4 100.2 %copy-start.24 = (pred[48,384]{1,0:T(8,128)(4,1)S(1)}, pred[48,384]{1,0:T(8,128)(4,1)}, u32[]{:S(2)}) copy-start(pred[48,384]{1,0:T(8,128)(4,1)} %iota_compare_fusion) | copy-start | bytes 55300
  438.5 246.6 %all-to-all-start.1 = ((bf16[408,24,384]{2,1,0:T(8,128)(2,1)}), bf16[408,24,384]{2,1,0:T(8,128)(2,1)}, u32[]{:S(2)}, u32[]{:S(2)}) async-start(bf16[408,24,384]{2,1,0:T(8,128)(2,1)} %slice_dynamic-update-slice_fusion.1), calls=%async_computation.1 | async-start | bytes 15040512 | tf_op jit(solution)/shard_map/all_to_all | solution.py:230
  443.4 8.8 copy-start.33
  447.5 197.0 %collective-permute-start = (bf16[24,192,384]{2,1,0:T(8,128)(2,1)}, bf16[24,192,384]{2,1,0:T(8,128)(2,1)}, u32[]{:S(2)}, u32[]{:S(2)}) collective-permute-start(bf16[24,192,384]{2,1,0:T(8,128)(2,1)} %slice_bitcast_fusion), channel_id=1, source_target_pairs={{0,7},{1,6},{2,5},{3,4},{4,3},{5,2},{6,1},{7,0},{8,15},{9,14},{10,... | collective-permute-start | bytes 10616840 | tf_op jit(solution)/shard_map/ppermute | solution.py:217
  1063.2 83.2 %all-to-all-start.5 = ((bf16[8,48,12,384]{3,1,2,0:T(8,128)(2,1)}), bf16[8,48,12,384]{3,1,2,0:T(8,128)(2,1)}, u32[]{:S(2)}, u32[]{:S(2)}) async-start(bf16[8,48,12,384]{3,1,2,0:T(8,128)(2,1)} %fusion.316), calls=%async_computation.5 | async-start | bytes 7077888 | tf_op jit(solution)/shard_map/all_to_all | solution.py:272
  1146.4 83.1 %all-to-all-start.3 = ((bf16[8,48,12,384]{3,1,2,0:T(8,128)(2,1)}), bf16[8,48,12,384]{3,1,2,0:T(8,128)(2,1)}, u32[]{:S(2)}, u32[]{:S(2)}) async-start(bf16[8,48,12,384]{3,1,2,0:T(8,128)(2,1)} %fusion.332), calls=%async_computation.3 | async-start | bytes 7077888 | tf_op jit(solution)/shard_map/all_to_all | solution.py:272
  1229.4 83.1 %all-to-all-start.6 = ((bf16[8,48,12,384]{3,1,2,0:T(8,128)(2,1)}), bf16[8,48,12,384]{3,1,2,0:T(8,128)(2,1)}, u32[]{:S(2)}, u32[]{:S(2)}) async-start(bf16[8,48,12,384]{3,1,2,0:T(8,128)(2,1)} %fusion.308), calls=%async_computation.6 | async-start | bytes 7077888 | tf_op jit(solution)/shard_map/all_to_all | solution.py:272
  1244.9 72.1 %copy-start.30 = (bf16[1,192]{1,0:T(2,128)(2,1)S(1)}, bf16[1,192]{1,0:T(2,128)(2,1)}, u32[]{:S(2)}) copy-start(bf16[1,192]{1,0:T(2,128)(2,1)} %param.17) | copy-start | bytes 1156
  1244.9 72.1 %copy-start.29 = (bf16[1,384]{1,0:T(2,128)(2,1)S(1)}, bf16[1,384]{1,0:T(2,128)(2,1)}, u32[]{:S(2)}) copy-start(bf16[1,384]{1,0:T(2,128)(2,1)} %param.19) | copy-start | bytes 2308
  1244.9 72.1 %copy-start.26 = (s32[384]{0:T(512)S(1)}, s32[384]{0:T(512)}, u32[]{:S(2)}) copy-start(s32[384]{0:T(512)} %copy-done.25) | copy-start | bytes 4612
  1312.5 106.1 %all-to-all-start.4 = ((bf16[8,48,12,384]{3,1,2,0:T(8,128)(2,1)}), bf16[8,48,12,384]{3,1,2,0:T(8,128)(2,1)}, u32[]{:S(2)}, u32[]{:S(2)}) async-start(bf16[8,48,12,384]{3,1,2,0:T(8,128)(2,1)} %fusion.324), calls=%async_computation.4 | async-start | bytes 7077888 | tf_op jit(solution)/shard_map/all_to_all | solution.py:272
  1396.4 3.6 copy-start.8
  1396.4 4.6 copy-start.23
  1406.1 3.6 copy-start.21
  1406.1 4.6 copy-start.22
  1447.5 3.6 copy-start.11
  1447.5 10.4 slice-start.2
  1451.1 6.9 slice-start.3
  1451.1 13.4 slice-start
  1458.0 6.5 slice-start.1
  1471.4 32.9 %copy-start.32 = (bf16[1,192,384]{2,1,0:T(8,128)(2,1)S(1)}, bf16[1,192,384]{2,1,0:T(8,128)(2,1)}, u32[]{:S(2)}) copy-start(bf16[1,192,384]{2,1,0:T(8,128)(2,1)} %param.20) | copy-start | bytes 442372
  1504.3 37.1 %copy-start.18 = (f32[12,768,384]{2,1,0:T(8,128)S(1)}, f32[12,768,384]{2,1,0:T(8,128)}, u32[]{:S(2)}) copy-start(f32[12,768,384]{2,1,0:T(8,128)} %fusion.266) | copy-start | bytes 42467332
  1541.4 109.5 %collective-permute-start.1 = (bf16[12,192,768]{2,1,0:T(8,128)(2,1)}, bf16[12,192,768]{2,1,0:T(8,128)(2,1)}, u32[]{:S(2)}, u32[]{:S(2)}) collective-permute-start(bf16[12,192,768]{2,1,0:T(8,128)(2,1)} %fusion.246), channel_id=1, source_target_pairs={{0,8},{8,16},{16,24},{24,0},{1,9},{9,17},{17,25},{25,1},{2,10},{10... | collective-permute-start | bytes 10616840 | tf_op jit(solution)/shard_map/ppermute | solution.py:18
  1541.4 38.6 %copy-start.10 = (f32[12,192,768]{2,1,0:T(8,128)S(1)}, f32[12,192,768]{2,1,0:T(8,128)}, u32[]{:S(2)}) copy-start(f32[12,192,768]{2,1,0:T(8,128)} %copy-done.9) | copy-start | bytes 21233668
  1541.4 38.6 %copy-start.17 = (f32[12,768,384]{2,1,0:T(8,128)S(1)}, f32[12,768,384]{2,1,0:T(8,128)}, u32[]{:S(2)}) copy-start(f32[12,768,384]{2,1,0:T(8,128)} %fusion.265) | copy-start | bytes 42467332
  1578.4 72.5 %collective-permute-start.4 = (bf16[12,192,768]{2,1,0:T(8,128)(2,1)}, bf16[12,192,768]{2,1,0:T(8,128)(2,1)}, u32[]{:S(2)}, u32[]{:S(2)}) collective-permute-start(bf16[12,192,768]{2,1,0:T(8,128)(2,1)} %fusion.243), channel_id=1, source_target_pairs={{0,8},{8,16},{16,24},{24,0},{1,9},{9,17},{17,25},{25,1},{2,10},{10... | collective-permute-start | bytes 10616840 | tf_op jit(solution)/shard_map/ppermute | solution.py:18
  1580.0 36.3 %copy-start.12 = (f32[12,192,768]{2,1,0:T(8,128)S(1)}, f32[12,192,768]{2,1,0:T(8,128)}, u32[]{:S(2)}) copy-start(f32[12,192,768]{2,1,0:T(8,128)} %copy-done.11) | copy-start | bytes 21233668
  1580.0 36.3 %copy-start.16 = (f32[12,768,384]{2,1,0:T(8,128)S(1)}, f32[12,768,384]{2,1,0:T(8,128)}, u32[]{:S(2)}) copy-start(f32[12,768,384]{2,1,0:T(8,128)} %fusion.264) | copy-start | bytes 42467332
  1580.0 36.3 %copy-start.34 = (u16[768,384]{1,0:T(8,128)(2,1)S(1)}, u16[768,384]{1,0:T(8,128)(2,1)}, u32[]{:S(2)}) copy-start(u16[768,384]{1,0:T(8,128)(2,1)} %get-tuple-element.786) | copy-start | bytes 1769476
  1580.0 36.3 %copy-start.35 = (u16[768,384]{1,0:T(8,128)(2,1)S(1)}, u16[768,384]{1,0:T(8,128)(2,1)}, u32[]{:S(2)}) copy-start(u16[768,384]{1,0:T(8,128)(2,1)} %get-tuple-element.787) | copy-start | bytes 1769476
  1616.2 42.1 %collective-permute-start.3 = (bf16[12,192,768]{2,1,0:T(8,128)(2,1)}, bf16[12,192,768]{2,1,0:T(8,128)(2,1)S(1)}, u32[]{:S(2)}, u32[]{:S(2)}) collective-permute-start(bf16[12,192,768]{2,1,0:T(8,128)(2,1)} %fusion.244), channel_id=1, source_target_pairs={{0,8},{8,16},{16,24},{24,0},{1,9},{9,17},{17,25},{25,1},{2,10},{10... | collective-permute-start | bytes 10616840 | tf_op jit(solution)/shard_map/ppermute | solution.py:18
  1650.2 46.1 %collective-permute-start.2 = (bf16[12,192,768]{2,1,0:T(8,128)(2,1)S(1)}, bf16[12,192,768]{2,1,0:T(8,128)(2,1)S(1)}, u32[]{:S(2)}, u32[]{:S(2)}) collective-permute-start(bf16[12,192,768]{2,1,0:T(8,128)(2,1)S(1)} %fusion.245), channel_id=1, source_target_pairs={{0,8},{8,16},{16,24},{24,0},{1,9},{9,17},{17,25},{25,1},{2,10},{10... | collective-permute-start | bytes 10616840 | tf_op jit(solution)/shard_map/ppermute | solution.py:18
  (9 other events, 21.8 us)
